TPU v7x, 32 devices: a whole 2x2x4 slice. The times are simulated.
32 devices in a mesh: gx: 8 (over y, x, core), gy: 4 (over z).
Axes of the slice: x: 2, y: 2, z: 4, core: 2. Of those that a mesh axis runs over, the one named last changes fastest.
Arguments:
- basis: float32 [32, 64, 32, 256], P(None, 'gx', 'gy'), may hold values from -6 to 6
- rhs: float32 [64, 32, 256], P('gx', 'gy'), may hold values from -12 to 12
- extra_diag: float32 [64, 32, 256], P('gx', 'gy'), may hold values from 0.02 to 0.5
- coeff: float32 [3, 64, 32, 256], P(None, 'gx', 'gy'), may hold values from 0.3 to 3
Outputs:
- guess: float32 [64, 32, 256], P('gx', 'gy')
- stepped: float32 [64, 32, 256], P('gx', 'gy')
All inputs are finite; a program needn't handle non-finite values.
Results may differ from a plain program's by a relative error of at most 0.0003.
Values sent between devices are 32-bit elements; how exact they have to be, the bound alone decides.
No kernel may reach another device: no remote copies, remote signals or barrier semaphores. Data moves between devices by JAX's collectives and lax.ppermute only.
A program may use at most 64 MiB of HBM per device.

v0:
```python
import jax
import jax.numpy as jnp
from jax import lax
from jax.sharding import PartitionSpec as P

precise = lax.Precision.HIGHEST


def shifted(block, axis, distance):
    devices = range(lax.axis_size(axis))
    route = [(i - distance, i) for i in devices if i - distance in devices]
    return lax.ppermute(block, axis, route)


def padded_2(cells, sides, width):
    for axis, dim in sides:
        count = lax.axis_size(axis)
        ends = count - 1
        head = lax.slice_in_dim(cells, 0, width, axis=dim)
        tail = lax.slice_in_dim(cells, cells.shape[dim] - width, cells.shape[dim], axis=dim)
        cells = jnp.concatenate(
            [
                lax.ppermute(tail, axis, [(i, (i + 1) % count) for i in range(ends)]),
                cells,
                lax.ppermute(head, axis, [((i + 1) % count, i) for i in range(ends)]),
            ],
            axis=dim,
        )
    return cells


def flux_apply(padded, coeff_pad, extra):
    center = padded[:, 1:-1, 1:-1]
    coeff_mid = coeff_pad[:, 1:-1, 1:-1]
    flux_x = coeff_mid[0] * (center - padded[:, 2:, 1:-1])
    flux_y = coeff_mid[1] * (center - padded[:, 1:-1, 2:])
    below_x = coeff_pad[0, :-2, 1:-1] * (padded[:, :-2, 1:-1] - center)
    below_y = coeff_pad[1, 1:-1, :-2] * (padded[:, 1:-1, :-2] - center)
    next_z = jnp.concatenate([center[..., 1:], jnp.zeros_like(center[..., :1])], axis=-1)
    flux_z = coeff_mid[2] * (center - next_z)
    below_z = jnp.concatenate([jnp.zeros_like(flux_z[..., :1]), flux_z[..., :-1]], axis=-1)
    return extra * center + flux_x + flux_y + flux_z - below_x - below_y - below_z


def small_solve(matrix, vector):
    lower = jnp.linalg.cholesky(matrix)
    middle = lax.linalg.triangular_solve(lower, vector[:, None], left_side=True, lower=True)
    result = lax.linalg.triangular_solve(
        lower, middle, left_side=True, lower=True, transpose_a=True
    )
    return result[:, 0]


def on_device(basis, rhs, extra_diag, coeff):
    lower_x = shifted(coeff[0][-1:], "gx", 1)
    lower_y = shifted(coeff[1][:, -1:], "gy", 1)
    coeff_pad = jnp.pad(coeff, ((0, 0), (1, 1), (1, 1), (0, 0)))
    coeff_pad = coeff_pad.at[0, 0, 1:-1].set(lower_x[0])
    coeff_pad = coeff_pad.at[1, 1:-1, 0].set(lower_y[:, 0])
    count = basis.shape[0]
    flat_basis = basis.reshape(count, -1)
    padded_basis = padded_2(basis, (("gx", 1), ("gy", 2)), 1)
    applied = flux_apply(padded_basis, coeff_pad, extra_diag)
    local_gram = jnp.dot(flat_basis, applied.reshape(count, -1).T, precision=precise)
    local_proj = jnp.dot(flat_basis, rhs.reshape(-1), precision=precise)
    gram, projected = lax.psum((local_gram, local_proj), ("gx", "gy"))
    gram = 0.5 * (gram + gram.T)
    weights = small_solve(gram, projected)
    guess = jnp.tensordot(weights, basis, axes=1, precision=precise)
    residual = rhs - jnp.tensordot(weights, applied, axes=1, precision=precise)
    coeff_mid = coeff_pad[:, 1:-1, 1:-1]
    below_kz = jnp.concatenate([jnp.zeros_like(coeff[2][..., :1]), coeff[2][..., :-1]], axis=-1)
    diagonal = (
        extra_diag
        + coeff_mid[0]
        + coeff_mid[1]
        + coeff_mid[2]
        + coeff_pad[0, :-2, 1:-1]
        + coeff_pad[1, 1:-1, :-2]
        + below_kz
    )
    direction = residual / diagonal
    direction_pad = padded_2(direction, (("gx", 0), ("gy", 1)), 1)
    applied_dir = flux_apply(direction_pad[None], coeff_pad, extra_diag)[0]
    local_corr = jnp.dot(flat_basis, applied_dir.reshape(-1), precision=precise)
    correction, numerator, curvature = lax.psum(
        (local_corr, jnp.sum(residual * direction), jnp.sum(direction * applied_dir)), ("gx", "gy")
    )
    shift_coef = small_solve(gram, correction)
    update = direction - jnp.tensordot(shift_coef, basis, axes=1, precision=precise)
    denominator = curvature - jnp.dot(correction, shift_coef, precision=precise)
    step_size = numerator / denominator
    return (guess, guess + step_size * update)


def solution(mesh):
    placed = (
        P(None, "gx", "gy", None),
        P("gx", "gy", None),
        P("gx", "gy", None),
        P(None, "gx", "gy", None),
    )
    return jax.shard_map(
        on_device,
        mesh=mesh,
        in_specs=placed,
        out_specs=(P("gx", "gy", None), P("gx", "gy", None)),
        check_vma=False,
    )
```

profile of v0, /device:TPU:0, one launch (start us, length us, event | category | flops | bytes accessed | tf_op | source)
XLA Modules:
  0.0 160.6 jit_solution(4980887315087795019)
XLA Ops:
  1.3 2.5 %collective-permute-start = (f32[1,8,256]{2,1,0:T(8,128)S(1)}, f32[1,8,256]{2,1,0:T(8,128)S(1)}, u32[]{:S(2)}, u32[]{:S(2)}) collective-permute-start(f32[1,8,256]{2,1,0:T(8,128)S(1)} %slice_bitcast_fusion.7), channel_id=1, source_target_pairs={{0,4},{4,8},{8,12},{12,16},{16,20},{20,24},{24,28},{1,5},{5,9},{9,... | collective-permute-start | bytes 24584 | tf_op jit(solution)/shard_map/ppermute | solution.py:12
  3.9 2.8 %copy.11 = f32[32,8,8,256]{3,0,2,1:T(8,128)S(1)} copy(f32[32,8,8,256]{3,2,1,0:T(8,128)} %param.13) | data formatting | bytes 4194304 | tf_op args[0]
  6.7 0.9 fusion.47
  7.6 4.5 %collective-permute-start.3 = (f32[32,1,8,256]{3,0,2,1:T(8,128)}, f32[32,1,8,256]{3,0,2,1:T(8,128)S(1)}, u32[]{:S(2)}, u32[]{:S(2)}) collective-permute-start(f32[32,1,8,256]{3,0,2,1:T(8,128)} %get-tuple-element.44), channel_id=1, source_target_pairs={{0,4},{4,8},{8,12},{12,16},{16,20},{20,24},{24,28},{1,5},{5,9},{9,... | collective-permute-start | bytes 786440 | tf_op jit(solution)/shard_map/ppermute | solution.py:23
  12.1 3.5 %collective-permute-start.1 = (f32[8,1,256]{2,1,0:T(1,128)S(1)}, f32[8,1,256]{2,1,0:T(1,128)S(1)}, u32[]{:S(2)}, u32[]{:S(2)}) collective-permute-start(f32[8,1,256]{2,1,0:T(1,128)S(1)} %slice.229), channel_id=1, source_target_pairs={{0,1},{1,2},{2,3},{4,5},{5,6},{6,7},{8,9},{9,10},{10,11},{12,13},{... | collective-permute-start | bytes 24584 | tf_op jit(solution)/shard_map/ppermute | solution.py:12
  15.6 1.4 collective-permute-start.2
  17.1 1.9 %slice.236 = f32[32,8,8,255]{3,0,2,1:T(8,128)} slice(f32[32,8,8,256]{3,0,2,1:T(8,128)S(1)} %copy.11), slice={[0:32], [0:8], [0:8], [1:256]} | slice | bytes 4177920 | tf_op jit(solution)/shard_map/slice | solution.py:39
  19.4 3.0 %subtract_multiply_fusion = (f32[32,8,8,256]{3,0,2,1:T(8,128)S(1)}, f32[32,10,8,256]{3,0,2,1:T(8,128)S(1)}) fusion(f32[32,8,8,255]{3,0,2,1:T(8,128)} %slice.236, f32[8,8,256]{2,1,0:T(8,128)S(1)} %get-tuple-element.48, f32[32,8,8,256]{3,2,1,0:T(8,128)S(1)} %copy-done, f32[32,10,8,256]{3,0,2,1:T(8,128)S(1)} %constant_dynamic-update-slice_fusion.2), kind=kLoop, calls=%fused_computation.18 | loop fusion | flops 1048576 | bytes 8445952 | tf_op jit(solution)/shard_map/mul | solution.py:40
  22.5 1.4 collective-permute-start.4
  24.0 4.6 %collective-permute-start.5 = (f32[32,10,1,256]{3,0,2,1:T(8,128)S(1)}, f32[32,10,1,256]{3,0,2,1:T(8,128)S(1)}, u32[]{:S(2)}, u32[]{:S(2)}) collective-permute-start(f32[32,10,1,256]{3,0,2,1:T(8,128)S(1)} %get-tuple-element.40), channel_id=1, source_target_pairs={{0,1},{1,2},{2,3},{4,5},{5,6},{6,7},{8,9},{9,10},{10,11},{12,13},{... | collective-permute-start | bytes 983048 | tf_op jit(solution)/shard_map/ppermute | solution.py:23
  28.5 2.8 %convolution_bitcast_fusion.5 = f32[32,1]{0,1:T(1,128)S(1)} fusion(f32[8,8,256,1]{2,1,0,3:T(8,128)S(1)} %bitcast.153, f32[32,8,8,256]{3,2,1,0:T(8,128)S(1)} %copy-done), kind=kOutput, calls=%fused_computation.24 | convolution fusion | flops 6291456 | bytes 2162816 | tf_op jit(solution)/shard_map/dot_general | solution.py:65
  31.3 3.7 %collective-permute-done.4 = f32[32,10,1,256]{3,0,2,1:T(8,128)S(1)} collective-permute-done((f32[32,10,1,256]{3,0,2,1:T(8,128)S(1)}, f32[32,10,1,256]{3,0,2,1:T(8,128)S(1)}, u32[]{:S(2)}, u32[]{:S(2)}) %collective-permute-start.4) | collective-permute-done | bytes 327712 | tf_op jit(solution)/shard_map/ppermute | solution.py:25
  35.0 1.5 collective-permute-done.5
  36.5 2.9 %fusion.3 = f32[32,8,8,256]{3,0,2,1:T(8,128)S(1)} fusion(f32[32,8,8,256]{3,0,2,1:T(8,128)S(1)} %copy-done.2, f32[32,10,8,256]{3,0,2,1:T(8,128)S(1)} %constant_dynamic-update-slice_fusion, f32[32,10,1,256]{3,0,2,1:T(8,128)S(1)} %collective-permute-done.5, f32[32,1,8,256]{3,0,2,1:T(8,128)S(1)} %collective-permute-done.3, ...), kind=kLoop, calls=%fused_computation.4 | loop fusion | flops 9961472 | bytes 12509184 | tf_op jit(solution)/shard_map/sub | solution.py:42
  39.4 1.3 copy-done.3
  40.7 2.9 %convolution_bitcast_fusion = f32[32,32]{1,0:T(8,128)S(1)} fusion(f32[32,8,8,256]{3,0,2,1:T(8,128)S(1)} %fusion.3, f32[32,8,8,256]{3,2,1,0:T(8,128)S(1)} %copy-done), kind=kOutput, calls=%fused_computation.19 | convolution fusion | flops 201326592 | bytes 4198400 | tf_op jit(solution)/shard_map/dot_general | solution.py:64
  43.6 40.9 %all-reduce.7 = (f32[32,1]{0,1:T(1,128)S(1)}, f32[32,32]{1,0:T(8,128)S(1)}) all-reduce(f32[32,1]{0,1:T(1,128)S(1)} %convolution_bitcast_fusion.5, f32[32,32]{1,0:T(8,128)S(1)} %convolution_bitcast_fusion), channel_id=1, replica_groups=mesh['gx'=8,'gy'=4] {'gx','gy'}, use_global_device_ids=true, to_apply=%region_3.0 | all-reduce | flops 1056 | bytes 8448 | tf_op jit(solution)/shard_map/psum | solution.py:66
  84.7 2.9 %cholesky.18 = f32[32,32]{1,0:T(8,128)S(1)} custom-call(f32[32,32]{1,0:T(8,128)S(1)} %fusion.34), custom_call_target="Cholesky" | custom-call | tf_op jit(solution)/shard_map/jit(cholesky)/cholesky | solution.py:46
  88.9 2.4 %custom-call.11 = f32[1,32,32]{1,2,0:T(8,128)S(1)} custom-call(f32[1,32,32]{2,1,0:T(8,128)S(1)} %fusion.28), custom_call_target="InvertDiagBlocksLowerTriangular" | custom-call | tf_op jit(solution)/shard_map/triangular_solve/custom-call.2 | solution.py:48
  91.7 2.7 %fusion.49 = f32[1,8,8,256]{3,0,2,1:T(1,128)S(1)} fusion(f32[32,1,1,1]{0,1,3,2:T(1,128)S(1)} %convolution_bitcast_fusion.2, f32[32,8,8,256]{3,0,2,1:T(8,128)} %copy-done.3), kind=kOutput, calls=%fused_computation.94 | convolution fusion | flops 6291456 | bytes 2162816 | tf_op jit(solution)/shard_map/dot_general | solution.py:70
  94.5 1.3 collective-permute-start.6
  95.8 1.3 collective-permute-start.7
  97.1 1.2 copy.40
  98.3 3.0 %collective-permute-done.7 = f32[1,8,256]{2,1,0:T(8,128)S(1)} collective-permute-done((f32[1,8,256]{2,1,0:T(8,128)S(1)}, f32[1,8,256]{2,1,0:T(8,128)S(1)}, u32[]{:S(2)}, u32[]{:S(2)}) %collective-permute-start.7) | collective-permute-done | bytes 8224 | tf_op jit(solution)/shard_map/ppermute | solution.py:25
  101.4 3.4 %collective-permute-start.8 = (f32[10,1,256]{2,1,0:T(1,128)S(1)}, f32[10,1,256]{2,1,0:T(1,128)S(1)}, u32[]{:S(2)}, u32[]{:S(2)}) collective-permute-start(f32[10,1,256]{2,1,0:T(1,128)S(1)} %get-tuple-element.52), channel_id=1, source_target_pairs={{0,1},{1,2},{2,3},{4,5},{5,6},{6,7},{8,9},{9,10},{10,11},{12,13},{... | collective-permute-start | bytes 30728 | tf_op jit(solution)/shard_map/ppermute | solution.py:23
  104.8 1.3 collective-permute-start.9
  106.1 2.2 %fusion.42 = f32[1,8,8,256]{3,0,2,1:T(1,128)S(1)} fusion(f32[32,1,1,1]{0,1,3,2:T(1,128)S(1)} %convolution_bitcast_fusion.2, f32[32,8,8,256]{3,2,1,0:T(8,128)S(1)} %copy-done), kind=kOutput, calls=%fused_computation.88 | convolution fusion | flops 6291456 | bytes 2162816 | tf_op jit(solution)/shard_map/dot_general | solution.py:69
  108.4 2.0 %collective-permute-done.9 = f32[10,1,256]{2,1,0:T(1,128)S(1)} collective-permute-done((f32[10,1,256]{2,1,0:T(1,128)S(1)}, f32[10,1,256]{2,1,0:T(1,128)S(1)}, u32[]{:S(2)}, u32[]{:S(2)}) %collective-permute-start.9) | collective-permute-done | bytes 10272 | tf_op jit(solution)/shard_map/ppermute | solution.py:25
  111.3 1.7 %convolution_bitcast_fusion.4 = f32[32]{0:T(128)S(1)} fusion(f32[16384,1]{0,1:T(1,128)S(1)} %bitcast.156, f32[32,16384]{1,0:T(8,128)S(1)} %bitcast.152), kind=kOutput, calls=%fused_computation.23 | convolution fusion | flops 6291456 | bytes 2162816 | tf_op jit(solution)/shard_map/dot_general | solution.py:85
  113.0 41.7 %all-reduce.6 = (f32[32]{0:T(128)S(1)}, f32[]{:T(128)}, f32[]{:T(128)}) all-reduce(f32[32]{0:T(128)S(1)} %convolution_bitcast_fusion.4, f32[]{:T(128)} %get-tuple-element.30, f32[]{:T(128)} %get-tuple-element.29), channel_id=1, replica_groups=mesh['gx'=8,'gy'=4] {'gx','gy'}, use_global_device_ids=true, to_apply=%region_8.12 | all-reduce | flops 34 | bytes 272 | tf_op jit(solution)/shard_map/psum | solution.py:86
  154.9 0.8 fusion.38
  155.7 2.2 %fusion.36 = f32[1,8,8,256]{3,0,2,1:T(1,128)S(1)} fusion(f32[1,32]{1,0:T(1,128)S(1)} %get-tuple-element.57, f32[32,8,8,256]{3,2,1,0:T(8,128)S(1)} %copy-done), kind=kOutput, calls=%fused_computation.81 | convolution fusion | flops 6291456 | bytes 2162816 | tf_op jit(solution)/shard_map/dot_general | solution.py:90
  (48 shorter events, 4.7 us)
Async XLA Ops:
  1.3 10.8 %copy-start.6 = (f32[3,8,8,256]{3,2,1,0:T(8,128)S(1)}, f32[3,8,8,256]{3,2,1,0:T(8,128)}, u32[]{:S(2)}) copy-start(f32[3,8,8,256]{3,2,1,0:T(8,128)} %param.16) | copy-start | bytes 589828
  1.3 17.7 %collective-permute-start = (f32[1,8,256]{2,1,0:T(8,128)S(1)}, f32[1,8,256]{2,1,0:T(8,128)S(1)}, u32[]{:S(2)}, u32[]{:S(2)}) collective-permute-start(f32[1,8,256]{2,1,0:T(8,128)S(1)} %slice_bitcast_fusion.7), channel_id=1, source_target_pairs={{0,4},{4,8},{8,12},{12,16},{16,20},{20,24},{24,28},{1,5},{5,9},{9,... | collective-permute-start | bytes 24584 | tf_op jit(solution)/shard_map/ppermute | solution.py:12
  6.7 12.3 %copy-start.1 = (f32[32,8,8,256]{3,0,2,1:T(8,128)}, f32[32,8,8,256]{3,0,2,1:T(8,128)S(1)}, u32[]{:S(2)}) copy-start(f32[32,8,8,256]{3,0,2,1:T(8,128)S(1)} %copy.11) | copy-start | bytes 6291460
  7.6 11.7 %collective-permute-start.3 = (f32[32,1,8,256]{3,0,2,1:T(8,128)}, f32[32,1,8,256]{3,0,2,1:T(8,128)S(1)}, u32[]{:S(2)}, u32[]{:S(2)}) collective-permute-start(f32[32,1,8,256]{3,0,2,1:T(8,128)} %get-tuple-element.44), channel_id=1, source_target_pairs={{0,4},{4,8},{8,12},{12,16},{16,20},{20,24},{24,28},{1,5},{5,9},{9,... | collective-permute-start | bytes 786440 | tf_op jit(solution)/shard_map/ppermute | solution.py:23
  12.1 7.1 %collective-permute-start.1 = (f32[8,1,256]{2,1,0:T(1,128)S(1)}, f32[8,1,256]{2,1,0:T(1,128)S(1)}, u32[]{:S(2)}, u32[]{:S(2)}) collective-permute-start(f32[8,1,256]{2,1,0:T(1,128)S(1)} %slice.229), channel_id=1, source_target_pairs={{0,1},{1,2},{2,3},{4,5},{5,6},{6,7},{8,9},{9,10},{10,11},{12,13},{... | collective-permute-start | bytes 24584 | tf_op jit(solution)/shard_map/ppermute | solution.py:12
  15.6 3.7 %copy-start = (f32[32,8,8,256]{3,2,1,0:T(8,128)S(1)}, f32[32,8,8,256]{3,2,1,0:T(8,128)}, u32[]{:S(2)}) copy-start(f32[32,8,8,256]{3,2,1,0:T(8,128)} %param.13) | copy-start | bytes 6291460
  15.6 6.8 %collective-permute-start.2 = (f32[32,1,8,256]{3,0,2,1:T(8,128)}, f32[32,1,8,256]{3,0,2,1:T(8,128)S(1)}, u32[]{:S(2)}, u32[]{:S(2)}) collective-permute-start(f32[32,1,8,256]{3,0,2,1:T(8,128)} %get-tuple-element.43), channel_id=1, source_target_pairs={{4,0},{8,4},{12,8},{16,12},{20,16},{24,20},{28,24},{5,1},{9,5},{13... | collective-permute-start | bytes 786440 | tf_op jit(solution)/shard_map/ppermute | solution.py:25
  19.4 9.2 %copy-start.5 = (f32[8,8,256]{2,1,0:T(8,128)S(1)}, f32[8,8,256]{2,1,0:T(8,128)}, u32[]{:S(2)}) copy-start(f32[8,8,256]{2,1,0:T(8,128)} %param.14) | copy-start | bytes 196612
  22.4 14.1 %copy-start.2 = (f32[32,8,8,256]{3,0,2,1:T(8,128)S(1)}, f32[32,8,8,256]{3,0,2,1:T(8,128)}, u32[]{:S(2)}) copy-start(f32[32,8,8,256]{3,0,2,1:T(8,128)} %copy-done.1) | copy-start | bytes 6291460
  22.4 14.1 %copy-start.4 = (f32[8,8,256]{2,1,0:T(8,128)S(1)}, f32[8,8,256]{2,1,0:T(8,128)}, u32[]{:S(2)}) copy-start(f32[8,8,256]{2,1,0:T(8,128)} %param.15) | copy-start | bytes 196612
  22.5 12.5 %collective-permute-start.4 = (f32[32,10,1,256]{3,0,2,1:T(8,128)S(1)}, f32[32,10,1,256]{3,0,2,1:T(8,128)S(1)}, u32[]{:S(2)}, u32[]{:S(2)}) collective-permute-start(f32[32,10,1,256]{3,0,2,1:T(8,128)S(1)} %get-tuple-element.39), channel_id=1, source_target_pairs={{1,0},{2,1},{3,2},{5,4},{6,5},{7,6},{9,8},{10,9},{11,10},{13,12},{... | collective-permute-start | bytes 983048 | tf_op jit(solution)/shard_map/ppermute | solution.py:25
  24.0 12.5 %collective-permute-start.5 = (f32[32,10,1,256]{3,0,2,1:T(8,128)S(1)}, f32[32,10,1,256]{3,0,2,1:T(8,128)S(1)}, u32[]{:S(2)}, u32[]{:S(2)}) collective-permute-start(f32[32,10,1,256]{3,0,2,1:T(8,128)S(1)} %get-tuple-element.40), channel_id=1, source_target_pairs={{0,1},{1,2},{2,3},{4,5},{5,6},{6,7},{8,9},{9,10},{10,11},{12,13},{... | collective-permute-start | bytes 983048 | tf_op jit(solution)/shard_map/ppermute | solution.py:23
  39.4 1.3 copy-start.3
  94.5 3.8 %collective-permute-start.6 = (f32[1,8,256]{2,1,0:T(8,128)S(1)}, f32[1,8,256]{2,1,0:T(8,128)S(1)}, u32[]{:S(2)}, u32[]{:S(2)}) collective-permute-start(f32[1,8,256]{2,1,0:T(8,128)S(1)} %get-tuple-element.54), channel_id=1, source_target_pairs={{0,4},{4,8},{8,12},{12,16},{16,20},{20,24},{24,28},{1,5},{5,9},{9,... | collective-permute-start | bytes 24584 | tf_op jit(solution)/shard_map/ppermute | solution.py:23
  95.8 5.6 %collective-permute-start.7 = (f32[1,8,256]{2,1,0:T(8,128)S(1)}, f32[1,8,256]{2,1,0:T(8,128)S(1)}, u32[]{:S(2)}, u32[]{:S(2)}) collective-permute-start(f32[1,8,256]{2,1,0:T(8,128)S(1)} %get-tuple-element.55), channel_id=1, source_target_pairs={{4,0},{8,4},{12,8},{16,12},{20,16},{24,20},{28,24},{5,1},{9,5},{13... | collective-permute-start | bytes 24584 | tf_op jit(solution)/shard_map/ppermute | solution.py:25
  101.4 7.0 %collective-permute-start.8 = (f32[10,1,256]{2,1,0:T(1,128)S(1)}, f32[10,1,256]{2,1,0:T(1,128)S(1)}, u32[]{:S(2)}, u32[]{:S(2)}) collective-permute-start(f32[10,1,256]{2,1,0:T(1,128)S(1)} %get-tuple-element.52), channel_id=1, source_target_pairs={{0,1},{1,2},{2,3},{4,5},{5,6},{6,7},{8,9},{9,10},{10,11},{12,13},{... | collective-permute-start | bytes 30728 | tf_op jit(solution)/shard_map/ppermute | solution.py:23
  104.8 5.6 %collective-permute-start.9 = (f32[10,1,256]{2,1,0:T(1,128)S(1)}, f32[10,1,256]{2,1,0:T(1,128)S(1)}, u32[]{:S(2)}, u32[]{:S(2)}) collective-permute-start(f32[10,1,256]{2,1,0:T(1,128)S(1)} %get-tuple-element.53), channel_id=1, source_target_pairs={{1,0},{2,1},{3,2},{5,4},{6,5},{7,6},{9,8},{10,9},{11,10},{13,12},{... | collective-permute-start | bytes 30728 | tf_op jit(solution)/shard_map/ppermute | solution.py:25
where the time goes:
time: 161 us
  blocking collectives  82.6 us (51%)
  starting transfers between devices  25.2 us (16%)
  matrix products  15.8 us (10%)
  other arithmetic  14.2 us (9%)
  waiting for transfers between devices  10.2 us (6%)
  local copies, waits for them, and re-layouts  9.6 us (6%)
  between operations  2.99 us (2%)
    psum x1, blocking collectives, on_device(): lax.psum((local_corr, jnp.sum(residual * direction), jnp.sum(direction *...  41.7 us
    psum x1, blocking collectives, on_device(): gram, projected = lax.psum((local_gram, local_proj), ('gx', 'gy'))  40.9 us
    ppermute x4, starting transfers between devices, padded_2(): lax.ppermute(tail, axis, [(i, (i + 1) % count) for i in range(ends)])  13.8 us
    ppermute x4, waiting for transfers between devices, padded_2(): lax.ppermute(head, axis, [((i + 1) % count, i) for i in range(ends)])  8.74 us
    ppermute x2, starting transfers between devices, shifted(): return lax.ppermute(block, axis, route)  6 us
    unnamed x18, local copies, waits for them, and re-layouts  5.48 us
    ppermute x4, starting transfers between devices, padded_2(): lax.ppermute(head, axis, [((i + 1) % count, i) for i in range(ends)])  5.43 us
    another operation x3, other arithmetic, small_solve(): lower = jnp.linalg.cholesky(matrix)  3.6 us
  transfers between devices with their start and end apart: 10, of which 4 were waited for; matrix products, arithmetic and copies ran while one was open for 9% of the time, Pallas kernels for 0%

commit v1 on v0

--- a/solution.py
+++ b/solution.py
@@ -84,7 +84,10 @@
     applied_dir = flux_apply(direction_pad[None], coeff_pad, extra_diag)[0]
     local_corr = jnp.dot(flat_basis, applied_dir.reshape(-1), precision=precise)
     correction, numerator, curvature = lax.psum(
-        (local_corr, jnp.sum(residual * direction), jnp.sum(direction * applied_dir)), ("gx", "gy")
+        lax.psum(
+            (local_corr, jnp.sum(residual * direction), jnp.sum(direction * applied_dir)), "gy"
+        ),
+        "gx",
     )
     shift_coef = small_solve(gram, correction)
     update = direction - jnp.tensordot(shift_coef, basis, axes=1, precision=precise)

time: 161 us -> 143 us (0.89)
  blocking collectives: 82.6 us -> 64.5 us
    psum x1, blocking collectives: 41.7 us -> 10.5 us  [on_device(): lax.psum((local_corr, jnp.sum(residual * direction), jnp.sum(direction *...]
    psum x0 -> x1, blocking collectives: none -> 13.1 us  [on_device(): lax.psum(lax.psum((local_corr, jnp.sum(residual * direction), jnp.sum(dir...]
  transfers between devices with their start and end apart: 10 -> 10, of which waited for: 4 -> 4; matrix products, arithmetic and copies ran while one was open for 9% -> 11% of each run, Pallas kernels for 0% -> 0%
where the time goes in v1:
time: 143 us
  blocking collectives  64.5 us (45%)
  starting transfers between devices  25.2 us (18%)
  matrix products  15.8 us (11%)
  other arithmetic  14.2 us (10%)
  waiting for transfers between devices  10.2 us (7%)
  local copies, waits for them, and re-layouts  9.62 us (7%)
  between operations  2.99 us (2%)
    psum x1, blocking collectives, on_device(): gram, projected = lax.psum((local_gram, local_proj), ('gx', 'gy'))  40.9 us
    ppermute x4, starting transfers between devices, padded_2(): lax.ppermute(tail, axis, [(i, (i + 1) % count) for i in range(ends)])  13.8 us
    psum x1, blocking collectives, on_device(): lax.psum(lax.psum((local_corr, jnp.sum(residual * direction), jnp.sum(dir...  13.1 us
    psum x1, blocking collectives, on_device(): lax.psum((local_corr, jnp.sum(residual * direction), jnp.sum(direction *...  10.5 us
    ppermute x4, waiting for transfers between devices, padded_2(): lax.ppermute(head, axis, [((i + 1) % count, i) for i in range(ends)])  8.74 us
    ppermute x2, starting transfers between devices, shifted(): return lax.ppermute(block, axis, route)  6 us
    unnamed x18, local copies, waits for them, and re-layouts  5.49 us
    ppermute x4, starting transfers between devices, padded_2(): lax.ppermute(head, axis, [((i + 1) % count, i) for i in range(ends)])  5.43 us
  transfers between devices with their start and end apart: 10, of which 4 were waited for; matrix products, arithmetic and copies ran while one was open for 11% of the time, Pallas kernels for 0%

profile of v1, /device:TPU:0, one launch (start us, length us, event | category | flops | bytes accessed | tf_op | source)
XLA Modules:
  0.0 142.5 jit_solution(980513942333689519)
XLA Ops:
  1.3 2.5 %collective-permute-start = (f32[1,8,256]{2,1,0:T(8,128)S(1)}, f32[1,8,256]{2,1,0:T(8,128)S(1)}, u32[]{:S(2)}, u32[]{:S(2)}) collective-permute-start(f32[1,8,256]{2,1,0:T(8,128)S(1)} %slice_bitcast_fusion.7), channel_id=1, source_target_pairs={{0,4},{4,8},{8,12},{12,16},{16,20},{20,24},{24,28},{1,5},{5,9},{9,... | collective-permute-start | bytes 24584 | tf_op jit(solution)/shard_map/ppermute | solution.py:12
  3.9 2.8 %copy.11 = f32[32,8,8,256]{3,0,2,1:T(8,128)S(1)} copy(f32[32,8,8,256]{3,2,1,0:T(8,128)} %param.13) | data formatting | bytes 4194304 | tf_op args[0]
  6.7 0.9 fusion.47
  7.6 4.5 %collective-permute-start.3 = (f32[32,1,8,256]{3,0,2,1:T(8,128)}, f32[32,1,8,256]{3,0,2,1:T(8,128)S(1)}, u32[]{:S(2)}, u32[]{:S(2)}) collective-permute-start(f32[32,1,8,256]{3,0,2,1:T(8,128)} %get-tuple-element.47), channel_id=1, source_target_pairs={{0,4},{4,8},{8,12},{12,16},{16,20},{20,24},{24,28},{1,5},{5,9},{9,... | collective-permute-start | bytes 786440 | tf_op jit(solution)/shard_map/ppermute | solution.py:23
  12.1 3.5 %collective-permute-start.1 = (f32[8,1,256]{2,1,0:T(1,128)S(1)}, f32[8,1,256]{2,1,0:T(1,128)S(1)}, u32[]{:S(2)}, u32[]{:S(2)}) collective-permute-start(f32[8,1,256]{2,1,0:T(1,128)S(1)} %slice.229), channel_id=1, source_target_pairs={{0,1},{1,2},{2,3},{4,5},{5,6},{6,7},{8,9},{9,10},{10,11},{12,13},{... | collective-permute-start | bytes 24584 | tf_op jit(solution)/shard_map/ppermute | solution.py:12
  15.6 1.4 collective-permute-start.2
  17.1 1.9 %slice.236 = f32[32,8,8,255]{3,0,2,1:T(8,128)} slice(f32[32,8,8,256]{3,0,2,1:T(8,128)S(1)} %copy.11), slice={[0:32], [0:8], [0:8], [1:256]} | slice | bytes 4177920 | tf_op jit(solution)/shard_map/slice | solution.py:39
  19.4 3.0 %subtract_multiply_fusion = (f32[32,8,8,256]{3,0,2,1:T(8,128)S(1)}, f32[32,10,8,256]{3,0,2,1:T(8,128)S(1)}) fusion(f32[32,8,8,255]{3,0,2,1:T(8,128)} %slice.236, f32[8,8,256]{2,1,0:T(8,128)S(1)} %get-tuple-element.51, f32[32,8,8,256]{3,2,1,0:T(8,128)S(1)} %copy-done, f32[32,10,8,256]{3,0,2,1:T(8,128)S(1)} %constant_dynamic-update-slice_fusion.2), kind=kLoop, calls=%fused_computation.18 | loop fusion | flops 1048576 | bytes 8445952 | tf_op jit(solution)/shard_map/mul | solution.py:40
  22.5 1.4 collective-permute-start.4
  24.0 4.6 %collective-permute-start.5 = (f32[32,10,1,256]{3,0,2,1:T(8,128)S(1)}, f32[32,10,1,256]{3,0,2,1:T(8,128)S(1)}, u32[]{:S(2)}, u32[]{:S(2)}) collective-permute-start(f32[32,10,1,256]{3,0,2,1:T(8,128)S(1)} %get-tuple-element.43), channel_id=1, source_target_pairs={{0,1},{1,2},{2,3},{4,5},{5,6},{6,7},{8,9},{9,10},{10,11},{12,13},{... | collective-permute-start | bytes 983048 | tf_op jit(solution)/shard_map/ppermute | solution.py:23
  28.6 2.8 %convolution_bitcast_fusion.5 = f32[32,1]{0,1:T(1,128)S(1)} fusion(f32[8,8,256,1]{2,1,0,3:T(8,128)S(1)} %bitcast.153, f32[32,8,8,256]{3,2,1,0:T(8,128)S(1)} %copy-done), kind=kOutput, calls=%fused_computation.24 | convolution fusion | flops 6291456 | bytes 2162816 | tf_op jit(solution)/shard_map/dot_general | solution.py:65
  31.3 3.7 %collective-permute-done.4 = f32[32,10,1,256]{3,0,2,1:T(8,128)S(1)} collective-permute-done((f32[32,10,1,256]{3,0,2,1:T(8,128)S(1)}, f32[32,10,1,256]{3,0,2,1:T(8,128)S(1)}, u32[]{:S(2)}, u32[]{:S(2)}) %collective-permute-start.4) | collective-permute-done | bytes 327712 | tf_op jit(solution)/shard_map/ppermute | solution.py:25
  35.0 1.5 %collective-permute-done.5 = f32[32,10,1,256]{3,0,2,1:T(8,128)S(1)} collective-permute-done((f32[32,10,1,256]{3,0,2,1:T(8,128)S(1)}, f32[32,10,1,256]{3,0,2,1:T(8,128)S(1)}, u32[]{:S(2)}, u32[]{:S(2)}) %collective-permute-start.5) | collective-permute-done | bytes 327712 | tf_op jit(solution)/shard_map/ppermute | solution.py:23
  36.5 2.9 %fusion.3 = f32[32,8,8,256]{3,0,2,1:T(8,128)S(1)} fusion(f32[32,8,8,256]{3,0,2,1:T(8,128)S(1)} %copy-done.2, f32[32,10,8,256]{3,0,2,1:T(8,128)S(1)} %constant_dynamic-update-slice_fusion, f32[32,10,1,256]{3,0,2,1:T(8,128)S(1)} %collective-permute-done.5, f32[32,1,8,256]{3,0,2,1:T(8,128)S(1)} %collective-permute-done.3, ...), kind=kLoop, calls=%fused_computation.4 | loop fusion | flops 9961472 | bytes 12509184 | tf_op jit(solution)/shard_map/sub | solution.py:42
  39.4 1.3 copy-done.3
  40.8 2.9 %convolution_bitcast_fusion = f32[32,32]{1,0:T(8,128)S(1)} fusion(f32[32,8,8,256]{3,0,2,1:T(8,128)S(1)} %fusion.3, f32[32,8,8,256]{3,2,1,0:T(8,128)S(1)} %copy-done), kind=kOutput, calls=%fused_computation.19 | convolution fusion | flops 201326592 | bytes 4198400 | tf_op jit(solution)/shard_map/dot_general | solution.py:64
  43.6 40.9 %all-reduce.6 = (f32[32,1]{0,1:T(1,128)S(1)}, f32[32,32]{1,0:T(8,128)S(1)}) all-reduce(f32[32,1]{0,1:T(1,128)S(1)} %convolution_bitcast_fusion.5, f32[32,32]{1,0:T(8,128)S(1)} %convolution_bitcast_fusion), channel_id=1, replica_groups=mesh['gx'=8,'gy'=4] {'gx','gy'}, use_global_device_ids=true, to_apply=%region_3.0 | all-reduce | flops 1056 | bytes 8448 | tf_op jit(solution)/shard_map/psum | solution.py:66
  84.7 2.9 %cholesky.18 = f32[32,32]{1,0:T(8,128)S(1)} custom-call(f32[32,32]{1,0:T(8,128)S(1)} %fusion.34), custom_call_target="Cholesky" | custom-call | tf_op jit(solution)/shard_map/jit(cholesky)/cholesky | solution.py:46
  88.9 2.4 %custom-call.11 = f32[1,32,32]{1,2,0:T(8,128)S(1)} custom-call(f32[1,32,32]{2,1,0:T(8,128)S(1)} %fusion.28), custom_call_target="InvertDiagBlocksLowerTriangular" | custom-call | tf_op jit(solution)/shard_map/triangular_solve/custom-call.2 | solution.py:48
  91.7 2.7 %fusion.49 = f32[1,8,8,256]{3,0,2,1:T(1,128)S(1)} fusion(f32[32,1,1,1]{0,1,3,2:T(1,128)S(1)} %convolution_bitcast_fusion.2, f32[32,8,8,256]{3,0,2,1:T(8,128)} %copy-done.3), kind=kOutput, calls=%fused_computation.94 | convolution fusion | flops 6291456 | bytes 2162816 | tf_op jit(solution)/shard_map/dot_general | solution.py:70
  94.5 1.3 collective-permute-start.6
  95.8 1.3 collective-permute-start.7
  97.1 1.2 copy.40
  98.3 3.0 %collective-permute-done.7 = f32[1,8,256]{2,1,0:T(8,128)S(1)} collective-permute-done((f32[1,8,256]{2,1,0:T(8,128)S(1)}, f32[1,8,256]{2,1,0:T(8,128)S(1)}, u32[]{:S(2)}, u32[]{:S(2)}) %collective-permute-start.7) | collective-permute-done | bytes 8224 | tf_op jit(solution)/shard_map/ppermute | solution.py:25
  101.4 3.4 %collective-permute-start.8 = (f32[10,1,256]{2,1,0:T(1,128)S(1)}, f32[10,1,256]{2,1,0:T(1,128)S(1)}, u32[]{:S(2)}, u32[]{:S(2)}) collective-permute-start(f32[10,1,256]{2,1,0:T(1,128)S(1)} %get-tuple-element.55), channel_id=1, source_target_pairs={{0,1},{1,2},{2,3},{4,5},{5,6},{6,7},{8,9},{9,10},{10,11},{12,13},{... | collective-permute-start | bytes 30728 | tf_op jit(solution)/shard_map/ppermute | solution.py:23
  104.8 1.3 collective-permute-start.9
  106.1 2.2 %fusion.42 = f32[1,8,8,256]{3,0,2,1:T(1,128)S(1)} fusion(f32[32,1,1,1]{0,1,3,2:T(1,128)S(1)} %convolution_bitcast_fusion.2, f32[32,8,8,256]{3,2,1,0:T(8,128)S(1)} %copy-done), kind=kOutput, calls=%fused_computation.88 | convolution fusion | flops 6291456 | bytes 2162816 | tf_op jit(solution)/shard_map/dot_general | solution.py:69
  108.4 2.0 %collective-permute-done.9 = f32[10,1,256]{2,1,0:T(1,128)S(1)} collective-permute-done((f32[10,1,256]{2,1,0:T(1,128)S(1)}, f32[10,1,256]{2,1,0:T(1,128)S(1)}, u32[]{:S(2)}, u32[]{:S(2)}) %collective-permute-start.9) | collective-permute-done | bytes 10272 | tf_op jit(solution)/shard_map/ppermute | solution.py:25
  111.3 1.7 %convolution_bitcast_fusion.4 = f32[32]{0:T(128)S(1)} fusion(f32[16384,1]{0,1:T(1,128)S(1)} %bitcast.156, f32[32,16384]{1,0:T(8,128)S(1)} %bitcast.152), kind=kOutput, calls=%fused_computation.23 | convolution fusion | flops 6291456 | bytes 2162816 | tf_op jit(solution)/shard_map/dot_general | solution.py:85
  113.0 10.5 %all-reduce.8 = (f32[32]{0:T(128)S(1)}, f32[]{:T(128)}, f32[]{:T(128)}) all-reduce(f32[32]{0:T(128)S(1)} %convolution_bitcast_fusion.4, f32[]{:T(128)} %get-tuple-element.30, f32[]{:T(128)} %get-tuple-element.29), channel_id=1, replica_groups=mesh['gx'=8,'gy'=4] {'gy'}, use_global_device_ids=true, to_apply=%region_10.14 | all-reduce | flops 34 | bytes 272 | tf_op jit(solution)/shard_map/psum | solution.py:87
  123.5 13.1 %all-reduce.7 = (f32[32]{0:T(128)S(1)}, f32[]{:T(128)}, f32[]{:T(128)}) all-reduce(f32[32]{0:T(128)S(1)} %get-tuple-element.36, f32[]{:T(128)} %get-tuple-element.37, f32[]{:T(128)} %get-tuple-element.38), channel_id=1, replica_groups=mesh['gx'=8,'gy'=4] {'gx'}, use_global_device_ids=true, to_apply=%region_11.15 | all-reduce | flops 34 | bytes 272 | tf_op jit(solution)/shard_map/psum | solution.py:86
  137.6 2.2 %fusion.36 = f32[1,8,8,256]{3,0,2,1:T(1,128)S(1)} fusion(f32[1,32]{1,0:T(1,128)S(1)} %get-tuple-element.60, f32[32,8,8,256]{3,2,1,0:T(8,128)S(1)} %copy-done), kind=kOutput, calls=%fused_computation.81 | convolution fusion | flops 6291456 | bytes 2162816 | tf_op jit(solution)/shard_map/dot_general | solution.py:93
  (49 shorter events, 5.6 us)
Async XLA Ops:
  1.3 10.8 %copy-start.6 = (f32[3,8,8,256]{3,2,1,0:T(8,128)S(1)}, f32[3,8,8,256]{3,2,1,0:T(8,128)}, u32[]{:S(2)}) copy-start(f32[3,8,8,256]{3,2,1,0:T(8,128)} %param.16) | copy-start | bytes 589828
  1.3 17.7 %collective-permute-start = (f32[1,8,256]{2,1,0:T(8,128)S(1)}, f32[1,8,256]{2,1,0:T(8,128)S(1)}, u32[]{:S(2)}, u32[]{:S(2)}) collective-permute-start(f32[1,8,256]{2,1,0:T(8,128)S(1)} %slice_bitcast_fusion.7), channel_id=1, source_target_pairs={{0,4},{4,8},{8,12},{12,16},{16,20},{20,24},{24,28},{1,5},{5,9},{9,... | collective-permute-start | bytes 24584 | tf_op jit(solution)/shard_map/ppermute | solution.py:12
  6.7 12.3 %copy-start.1 = (f32[32,8,8,256]{3,0,2,1:T(8,128)}, f32[32,8,8,256]{3,0,2,1:T(8,128)S(1)}, u32[]{:S(2)}) copy-start(f32[32,8,8,256]{3,0,2,1:T(8,128)S(1)} %copy.11) | copy-start | bytes 6291460
  7.6 11.8 %collective-permute-start.3 = (f32[32,1,8,256]{3,0,2,1:T(8,128)}, f32[32,1,8,256]{3,0,2,1:T(8,128)S(1)}, u32[]{:S(2)}, u32[]{:S(2)}) collective-permute-start(f32[32,1,8,256]{3,0,2,1:T(8,128)} %get-tuple-element.47), channel_id=1, source_target_pairs={{0,4},{4,8},{8,12},{12,16},{16,20},{20,24},{24,28},{1,5},{5,9},{9,... | collective-permute-start | bytes 786440 | tf_op jit(solution)/shard_map/ppermute | solution.py:23
  12.1 7.1 %collective-permute-start.1 = (f32[8,1,256]{2,1,0:T(1,128)S(1)}, f32[8,1,256]{2,1,0:T(1,128)S(1)}, u32[]{:S(2)}, u32[]{:S(2)}) collective-permute-start(f32[8,1,256]{2,1,0:T(1,128)S(1)} %slice.229), channel_id=1, source_target_pairs={{0,1},{1,2},{2,3},{4,5},{5,6},{6,7},{8,9},{9,10},{10,11},{12,13},{... | collective-permute-start | bytes 24584 | tf_op jit(solution)/shard_map/ppermute | solution.py:12
  15.6 3.7 %copy-start = (f32[32,8,8,256]{3,2,1,0:T(8,128)S(1)}, f32[32,8,8,256]{3,2,1,0:T(8,128)}, u32[]{:S(2)}) copy-start(f32[32,8,8,256]{3,2,1,0:T(8,128)} %param.13) | copy-start | bytes 6291460
  15.6 6.8 %collective-permute-start.2 = (f32[32,1,8,256]{3,0,2,1:T(8,128)}, f32[32,1,8,256]{3,0,2,1:T(8,128)S(1)}, u32[]{:S(2)}, u32[]{:S(2)}) collective-permute-start(f32[32,1,8,256]{3,0,2,1:T(8,128)} %get-tuple-element.46), channel_id=1, source_target_pairs={{4,0},{8,4},{12,8},{16,12},{20,16},{24,20},{28,24},{5,1},{9,5},{13... | collective-permute-start | bytes 786440 | tf_op jit(solution)/shard_map/ppermute | solution.py:25
  19.4 9.2 %copy-start.5 = (f32[8,8,256]{2,1,0:T(8,128)S(1)}, f32[8,8,256]{2,1,0:T(8,128)}, u32[]{:S(2)}) copy-start(f32[8,8,256]{2,1,0:T(8,128)} %param.14) | copy-start | bytes 196612
  22.4 14.1 %copy-start.2 = (f32[32,8,8,256]{3,0,2,1:T(8,128)S(1)}, f32[32,8,8,256]{3,0,2,1:T(8,128)}, u32[]{:S(2)}) copy-start(f32[32,8,8,256]{3,0,2,1:T(8,128)} %copy-done.1) | copy-start | bytes 6291460
  22.4 14.1 %copy-start.4 = (f32[8,8,256]{2,1,0:T(8,128)S(1)}, f32[8,8,256]{2,1,0:T(8,128)}, u32[]{:S(2)}) copy-start(f32[8,8,256]{2,1,0:T(8,128)} %param.15) | copy-start | bytes 196612
  22.5 12.5 %collective-permute-start.4 = (f32[32,10,1,256]{3,0,2,1:T(8,128)S(1)}, f32[32,10,1,256]{3,0,2,1:T(8,128)S(1)}, u32[]{:S(2)}, u32[]{:S(2)}) collective-permute-start(f32[32,10,1,256]{3,0,2,1:T(8,128)S(1)} %get-tuple-element.42), channel_id=1, source_target_pairs={{1,0},{2,1},{3,2},{5,4},{6,5},{7,6},{9,8},{10,9},{11,10},{13,12},{... | collective-permute-start | bytes 983048 | tf_op jit(solution)/shard_map/ppermute | solution.py:25
  24.0 12.5 %collective-permute-start.5 = (f32[32,10,1,256]{3,0,2,1:T(8,128)S(1)}, f32[32,10,1,256]{3,0,2,1:T(8,128)S(1)}, u32[]{:S(2)}, u32[]{:S(2)}) collective-permute-start(f32[32,10,1,256]{3,0,2,1:T(8,128)S(1)} %get-tuple-element.43), channel_id=1, source_target_pairs={{0,1},{1,2},{2,3},{4,5},{5,6},{6,7},{8,9},{9,10},{10,11},{12,13},{... | collective-permute-start | bytes 983048 | tf_op jit(solution)/shard_map/ppermute | solution.py:23
  39.4 1.4 copy-start.3
  94.5 3.8 %collective-permute-start.6 = (f32[1,8,256]{2,1,0:T(8,128)S(1)}, f32[1,8,256]{2,1,0:T(8,128)S(1)}, u32[]{:S(2)}, u32[]{:S(2)}) collective-permute-start(f32[1,8,256]{2,1,0:T(8,128)S(1)} %get-tuple-element.57), channel_id=1, source_target_pairs={{0,4},{4,8},{8,12},{12,16},{16,20},{20,24},{24,28},{1,5},{5,9},{9,... | collective-permute-start | bytes 24584 | tf_op jit(solution)/shard_map/ppermute | solution.py:23
  95.8 5.6 %collective-permute-start.7 = (f32[1,8,256]{2,1,0:T(8,128)S(1)}, f32[1,8,256]{2,1,0:T(8,128)S(1)}, u32[]{:S(2)}, u32[]{:S(2)}) collective-permute-start(f32[1,8,256]{2,1,0:T(8,128)S(1)} %get-tuple-element.58), channel_id=1, source_target_pairs={{4,0},{8,4},{12,8},{16,12},{20,16},{24,20},{28,24},{5,1},{9,5},{13... | collective-permute-start | bytes 24584 | tf_op jit(solution)/shard_map/ppermute | solution.py:25
  101.4 7.0 %collective-permute-start.8 = (f32[10,1,256]{2,1,0:T(1,128)S(1)}, f32[10,1,256]{2,1,0:T(1,128)S(1)}, u32[]{:S(2)}, u32[]{:S(2)}) collective-permute-start(f32[10,1,256]{2,1,0:T(1,128)S(1)} %get-tuple-element.55), channel_id=1, source_target_pairs={{0,1},{1,2},{2,3},{4,5},{5,6},{6,7},{8,9},{9,10},{10,11},{12,13},{... | collective-permute-start | bytes 30728 | tf_op jit(solution)/shard_map/ppermute | solution.py:23
  104.8 5.6 %collective-permute-start.9 = (f32[10,1,256]{2,1,0:T(1,128)S(1)}, f32[10,1,256]{2,1,0:T(1,128)S(1)}, u32[]{:S(2)}, u32[]{:S(2)}) collective-permute-start(f32[10,1,256]{2,1,0:T(1,128)S(1)} %get-tuple-element.56), channel_id=1, source_target_pairs={{1,0},{2,1},{3,2},{5,4},{6,5},{7,6},{9,8},{10,9},{11,10},{13,12},{... | collective-permute-start | bytes 30728 | tf_op jit(solution)/shard_map/ppermute | solution.py:25
